TPU v7x, 256 devices: a whole 4x4x8 slice. The times are simulated.
256 devices in a mesh: group: 32 (over x, y, core), mp: 8 (over z).
Axes of the slice: x: 4, y: 4, z: 8, core: 2. Of those that a mesh axis runs over, the one named last changes fastest.
Arguments:
- hidden: bfloat16 [16384, 1792], P('group')
- norm_gain: float32 [1792], replicated, may hold values from 0.1 to 1.9
- qkv_weight: bfloat16 [1792, 2304], P(None, 'mp'), may hold values from -0.125 to 0.125
- out_weight: bfloat16 [1792, 1792], P('mp'), may hold values from -0.125 to 0.125
- adapter_down: bfloat16 [1792, 1024], P(None, 'mp'), may hold values from -0.125 to 0.125
- adapter_up: bfloat16 [1024, 1792], P('mp'), may hold values from -1.5 to 1.5
- vocab_rows: bfloat16 [4096, 1792], P(('group', 'mp')), may hold values from -0.125 to 0.125
- segments: int32 [16384], P('group'), may hold values from 0 to 127, never falling along the last dimension, each value on 1 to 512 neighbouring positions
- request_adapter: int32 [128], replicated, may hold values from 0 to 63
- adapter_slot: int32 [64], replicated, may hold values from 0 to 63, each once
- page_table: int32 [2048], replicated, may hold values from 0 to 2047, as said below
Outputs:
- layer_update: bfloat16 [16384, 1792], P('group', 'mp')
- state_norms: float32 [16, 16384], P('mp', 'group')
- max_logits: float32 [16384], P(('group', 'mp'))
Inputs may be any that keep to these rules, and one draw needn't show every extreme that they name: A permutation of all pages. Logical page k of group g (entry g * 64 + k) lies in group page_table[g * 64 + k] // 64, and every group holds exactly two of the logical pages of every group. `segments`: every request's tokens stand together and in order; no request has more than 512 tokens. `adapter_slot`: A permutation.
All inputs are finite; a program needn't handle non-finite values.
Results may differ from a plain program's by a relative error of at most 0.013.
Values may be sent and summed in bfloat16 or wider, within the bound.
A program may use at most 64 MiB of HBM per device.

v0:
```python
import jax
import jax.numpy as jnp
from jax import lax
from jax.sharding import PartitionSpec as P

FEAT = 16
HD = 112
RANK = 16
EPSILON = 1e-05
PRECISE = lax.Precision.HIGHEST


def from_behind(value, axis, by):
    size = lax.axis_size(axis)
    pairs = [(i, i + by) for i in range(size) if 0 <= i + by < size]
    return lax.ppermute(value, axis, pairs)


def rms_normed(values, norm_gain):
    wide = values.astype(jnp.float32)
    meansq = jnp.mean(wide * wide, axis=-1, keepdims=True)
    return (wide * lax.rsqrt(meansq + EPSILON) * norm_gain).astype(jnp.bfloat16)


def features(vectors, feat_width):
    linear_part = vectors / feat_width**0.25
    outer_part = (vectors[..., :, None] * vectors[..., None, :]).reshape(
        vectors.shape[:-1] + (feat_width * feat_width,)
    )
    outer_part = outer_part / (2.0 * feat_width) ** 0.5
    ones_part = jnp.ones(vectors.shape[:-1] + (1,), jnp.float32)
    return jnp.concatenate([ones_part, linear_part, outer_part], axis=-1)


def block_step(state_carry, block_inputs, feat_width):
    states, totals, owner_seg = state_carry
    phi_query, phi_key, query_rows, key_rows, value_rows, seg_ids = block_inputs
    scaling = feat_width ** (-0.5)
    block_len = seg_ids.shape[0]
    position = jnp.arange(block_len, dtype=jnp.int32)
    allowed = (
        (position[:, None] >= position[None, :]) & (seg_ids[:, None] == seg_ids[None, :])
    ).astype(jnp.float32)
    carried = (seg_ids == owner_seg).astype(jnp.float32)[None, :]
    scores = jnp.einsum("hcf,hdf->hcd", query_rows, key_rows, precision=PRECISE) * scaling
    weights = (1.0 + scores + 0.5 * scores * scores) * allowed[None]
    numerator = jnp.einsum("hcd,hde->hce", weights, value_rows, precision=PRECISE)
    numerator = numerator + carried[..., None] * jnp.einsum(
        "hcp,hpe->hce", phi_query, states, precision=PRECISE
    )
    denominator = jnp.sum(weights, axis=-1) + carried * jnp.einsum(
        "hcp,hp->hc", phi_query, totals, precision=PRECISE
    )
    mixed_out = numerator / denominator[..., None]
    key_scores = jnp.einsum("hcf,hdf->hcd", key_rows, key_rows, precision=PRECISE) * scaling
    value_gram = jnp.einsum("hce,hde->hcd", value_rows, value_rows, precision=PRECISE)
    key_gram = (1.0 + key_scores + 0.5 * key_scores * key_scores) * value_gram
    masked_gram = jnp.einsum("cd,hde->hce", allowed, key_gram, precision=PRECISE)
    local_squares = jnp.sum(masked_gram * allowed[None], axis=-1)
    along = jnp.sum(
        jnp.einsum("hcp,hpe->hce", phi_key, states, precision=PRECISE) * value_rows, axis=-1
    )
    cross_squares = jnp.einsum("cd,hd->hc", allowed, along, precision=PRECISE)
    state_squares = jnp.sum(states * states, axis=(1, 2))
    squares = carried * (state_squares[:, None] + 2.0 * cross_squares) + local_squares
    counted = carried * totals[:, :1] + jnp.sum(allowed, axis=-1)[None, :]
    state_norm = jnp.sqrt(squares / (counted * (feat_width * value_rows.shape[-1])))
    last_seg = seg_ids[-1]
    member = (seg_ids == last_seg).astype(jnp.float32)
    continues = (owner_seg == last_seg).astype(jnp.float32)
    new_states = continues * states + jnp.einsum(
        "hcp,hce->hpe", phi_key * member[None, :, None], value_rows, precision=PRECISE
    )
    new_totals = continues * totals + jnp.einsum("hcp,c->hp", phi_key, member, precision=PRECISE)
    return ((new_states, new_totals, last_seg), (mixed_out, state_norm))


def best_of(candidates, piece):
    logits = jnp.einsum("rd,vd->rv", candidates, piece, preferred_element_type=jnp.float32)
    return jnp.max(logits, axis=1)


def on_device(
    hidden,
    norm_gain,
    qkv_weight,
    out_weight,
    adapter_down,
    adapter_up,
    vocab_rows,
    segments,
    request_adapter,
    adapter_slot,
    page_table,
):
    groups = lax.axis_size("group")
    own_group = lax.axis_index("group")
    shards = lax.axis_size("mp")
    own_shard = lax.axis_index("mp")
    rows_here = segments.shape[0]
    model_width = hidden.shape[1]
    slice_width = model_width // shards
    table = page_table.reshape(groups, -1)
    per_group = table.shape[1]
    per_peer = per_group // groups
    page_len = rows_here // per_group
    holders = table // per_group
    position = jnp.arange(per_group, dtype=jnp.int32)
    sort_keys = jnp.where(holders == own_group, position[None, :], per_group + position[None, :])
    ranked = jnp.argsort(sort_keys, axis=1)[:, :per_peer]
    picked = jnp.take_along_axis(table, ranked, axis=1) - own_group * per_group
    outgoing = hidden.reshape(per_group, page_len, model_width)[picked]
    normed_pages = rms_normed(outgoing, norm_gain)
    projected_pages = jnp.einsum(
        "abrd,dc->abrc", normed_pages, qkv_weight, preferred_element_type=jnp.float32
    ).astype(jnp.bfloat16)
    lowered_pages = jnp.einsum(
        "abrd,dc->abrc", normed_pages, adapter_down, preferred_element_type=jnp.float32
    ).astype(jnp.bfloat16)
    kept_pages = lax.dynamic_slice_in_dim(outgoing, own_shard * slice_width, slice_width, 3)
    arrived = (
        lax.all_to_all(kept_pages, "group", split_axis=0, concat_axis=0, tiled=True),
        lax.all_to_all(projected_pages, "group", split_axis=0, concat_axis=0, tiled=True),
        lax.all_to_all(lowered_pages, "group", split_axis=0, concat_axis=0, tiled=True),
    )
    own_holders = lax.dynamic_index_in_dim(holders, own_group, 0, keepdims=False)
    onehot = (own_holders[:, None] == jnp.arange(groups, dtype=jnp.int32)[None, :]).astype(
        jnp.int32
    )
    earlier = jnp.sum((jnp.cumsum(onehot, axis=0) - onehot) * onehot, axis=1)
    source_rows = own_holders * per_peer + earlier

    def placed(received):
        gathered_rows = received.reshape((groups * per_peer,) + received.shape[2:])[source_rows]
        return gathered_rows.reshape((rows_here,) + received.shape[3:])

    residual, projected, lowered = [placed(received) for received in arrived]
    group_vocab = lax.all_gather(vocab_rows, "group", axis=0, tiled=True)
    group_vocab, projected = lax.optimization_barrier((group_vocab, projected))
    heads_here = projected.shape[1] // (2 * FEAT + HD)
    split_heads = jnp.transpose(
        projected.reshape(rows_here, heads_here, 2 * FEAT + HD).astype(jnp.float32), (1, 0, 2)
    )
    query_rows = split_heads[..., :FEAT]
    key_rows = split_heads[..., FEAT : 2 * FEAT]
    value_rows = split_heads[..., 2 * FEAT :]
    phi_query = features(query_rows, FEAT)
    phi_key = features(key_rows, FEAT)
    last_seg = segments[-1]
    member = (segments == last_seg).astype(jnp.float32)
    end_state = jnp.einsum(
        "hcp,hce->hpe", phi_key * member[None, :, None], value_rows, precision=PRECISE
    )
    end_totals = jnp.einsum("hcp,c->hp", phi_key, member, precision=PRECISE)
    end_tag = jnp.reshape(last_seg + 1, (1,)).astype(jnp.float32)
    got_state, got_totals, got_tag = (
        from_behind(end_state.astype(jnp.bfloat16), "group", 1).astype(end_state.dtype),
        from_behind(end_totals.astype(jnp.bfloat16), "group", 1).astype(end_totals.dtype),
        from_behind(end_tag.astype(jnp.bfloat16), "group", 1).astype(end_tag.dtype),
    )
    initial = (got_state, got_totals, got_tag[0].astype(jnp.int32) - 1)
    block_len = min(256, rows_here)
    blocks = rows_here // block_len

    def regroup(values):
        return jnp.transpose(
            values.reshape(values.shape[0], blocks, block_len, values.shape[-1]), (1, 0, 2, 3)
        )

    scan_inputs = (
        regroup(phi_query),
        regroup(phi_key),
        regroup(query_rows),
        regroup(key_rows),
        regroup(value_rows),
        segments.reshape(blocks, block_len),
    )

    def scan_step(state_carry, block_inputs):
        return block_step(state_carry, block_inputs, FEAT)

    _, (mixed_out, state_norm) = lax.scan(scan_step, initial, scan_inputs)
    attended = (
        jnp.transpose(mixed_out, (0, 2, 1, 3))
        .reshape(rows_here, heads_here * HD)
        .astype(jnp.bfloat16)
    )
    state_norms = jnp.transpose(state_norm, (1, 0, 2)).reshape(heads_here, rows_here)
    request_ids = jnp.arange(request_adapter.shape[0], dtype=jnp.int32)
    adapter_of = jnp.sum(
        jnp.where(segments[:, None] == request_ids[None, :], request_adapter[None, :], 0), axis=1
    )
    adapter_ids = jnp.arange(adapter_slot.shape[0], dtype=jnp.int32)
    slot_ids = jnp.sum(
        jnp.where(adapter_of[:, None] == adapter_ids[None, :], adapter_slot[None, :], 0), axis=1
    )
    column_slot = jnp.arange(lowered.shape[1], dtype=jnp.int32) // RANK
    local_slot = slot_ids - own_shard * (lowered.shape[1] // RANK)
    low_rank = jnp.where(
        local_slot[:, None] == column_slot[None, :], lowered, jnp.zeros_like(lowered)
    )
    partial_value = jnp.dot(attended, out_weight, preferred_element_type=jnp.float32)
    partial_value = partial_value + jnp.dot(
        low_rank, adapter_up, preferred_element_type=jnp.float32
    )
    summed = lax.psum_scatter(
        partial_value.astype(jnp.bfloat16), "mp", scatter_dimension=1, tiled=True
    )
    final_rows = (residual.astype(jnp.float32) + summed.astype(jnp.float32)).astype(jnp.bfloat16)
    group_rows = lax.all_gather(final_rows, "mp", axis=1, tiled=True)
    partial_best = best_of(group_rows, group_vocab)
    max_logits = lax.dynamic_slice_in_dim(
        lax.pmax(partial_best, "mp"), own_shard * (rows_here // shards), rows_here // shards
    )
    return (summed, state_norms, max_logits)


def solution(mesh):
    placed = (
        P("group", None),
        P(),
        P(None, "mp"),
        P("mp", None),
        P(None, "mp"),
        P("mp", None),
        P(("group", "mp"), None),
        P("group"),
        P(),
        P(),
        P(),
    )
    return jax.shard_map(
        on_device,
        mesh=mesh,
        in_specs=placed,
        out_specs=(P("group", "mp"), P("mp", "group"), P(("group", "mp"))),
        check_vma=False,
    )
```

profile of v0, /device:TPU:2, one launch (start us, length us, event | category | flops | bytes accessed | tf_op | source)
XLA Modules:
  0.0 222.2 jit_solution(6068181078464134090)
XLA Ops:
  7.9 1.3 slice.34
  9.8 2.7 %collective-permute-start.2 = (bf16[1]{0:T(256)(128)(2,1)}, bf16[1]{0:T(256)(128)(2,1)}, u32[]{:S(2)}, u32[]{:S(2)}) collective-permute-start(bf16[1]{0:T(256)(128)(2,1)} %bitcast.33), channel_id=1, source_target_pairs={{0,8},{8,16},{16,24},{24,32},{32,40},{40,48},{48,56},{56,64},{64,7... | collective-permute-start | bytes 14 | tf_op jit(solution)/shard_map/ppermute | solution.py:16
  15.9 1.9 gather_fusion
  17.8 2.0 fusion.49
  20.0 3.0 %fusion.59 = bf16[32,2,8,128]{3,2,1,0:T(8,128)(2,1)} fusion(bf16[32,2,8,1792]{3,2,1,0:T(8,128)(2,1)} %bitcast.226, f32[1792]{0:T(1024)S(1)} %copy-done.14, f32[32,2,8]{2,1,0:T(2,128)S(1)} %copy.89, bf16[1792,128]{1,0:T(8,128)(2,1)} %param.17), kind=kOutput, calls=%fused_computation.84 | convolution fusion | flops 238616576 | bytes 2434048 | tf_op jit(solution)/shard_map/abrd,dc->abrc/dot_general | solution.py:117
  23.0 8.5 %all-to-all-start.1 = ((bf16[32,2,8,128]{3,2,1,0:T(8,128)(2,1)}), bf16[32,2,8,128]{3,2,1,0:T(8,128)(2,1)S(1)}, u32[]{:S(2)}, u32[]{:S(2)}) async-start(bf16[32,2,8,128]{3,2,1,0:T(8,128)(2,1)} %fusion.59), calls=%async_computation.1 | async-start | bytes 262144 | tf_op jit(solution)/shard_map/all_to_all | solution.py:124
  32.8 3.4 %fusion.56 = bf16[32,2,8,288]{3,2,1,0:T(8,128)(2,1)} fusion(bf16[32,2,8,1792]{3,2,1,0:T(8,128)(2,1)} %bitcast.227, f32[1792]{0:T(1024)S(1)} %copy-done.14, f32[32,2,8]{2,1,0:T(2,128)S(1)} %copy.89, bf16[1792,288]{0,1:T(8,128)(2,1)S(1)} %copy-done.13), kind=kOutput, calls=%fused_computation.81 | convolution fusion | flops 532299776 | bytes 3171328 | tf_op jit(solution)/shard_map/abrd,dc->abrc/dot_general | solution.py:114
  36.4 1.8 all-to-all-done.1
  38.2 5.6 %all-to-all-start = ((bf16[32,2,8,288]{3,2,1,0:T(8,128)(2,1)}), bf16[32,2,8,288]{3,2,1,0:T(8,128)(2,1)S(1)}, u32[]{:S(2)}, u32[]{:S(2)}) async-start(bf16[32,2,8,288]{3,2,1,0:T(8,128)(2,1)} %fusion.56), calls=%async_computation | async-start | bytes 786432 | tf_op jit(solution)/shard_map/all_to_all | solution.py:123
  45.1 1.3 gather_fusion.2
  46.4 6.2 %all-to-all-done = bf16[32,2,8,288]{3,2,1,0:T(8,128)(2,1)S(1)} async-done(((bf16[32,2,8,288]{3,2,1,0:T(8,128)(2,1)}), bf16[32,2,8,288]{3,2,1,0:T(8,128)(2,1)S(1)}, u32[]{:S(2)}, u32[]{:S(2)}) %all-to-all-start) | async-done | bytes 294944 | tf_op jit(solution)/shard_map/all_to_all | solution.py:123
  53.2 9.2 %all-gather.3.cloned.1.call-done = bf16[512,1792]{1,0:T(8,128)(2,1)} async-done(((bf16[16,1792]{1,0:T(8,128)(2,1)}), bf16[512,1792]{1,0:T(8,128)(2,1)}) %all-gather.3.cloned.1.call-update) | async-done | bytes 1835024 | tf_op jit(solution)/shard_map/all_gather | solution.py:138
  63.0 1.3 pad_maximum_fusion.1
  64.3 1.3 convolution_convert_fusion
  66.5 2.2 collective-permute-start.1
  68.6 2.4 %collective-permute-start = (bf16[2,273,112]{2,1,0:T(8,128)(2,1)}, bf16[2,273,112]{2,1,0:T(8,128)(2,1)}, u32[]{:S(2)}, u32[]{:S(2)}) collective-permute-start(bf16[2,273,112]{2,1,0:T(8,128)(2,1)} %convolution_convert_fusion), channel_id=1, source_target_pairs={{0,8},{8,16},{16,24},{24,32},{32,40},{40,48},{48,56},{56,64},{64,7... | collective-permute-start | bytes 366920 | tf_op jit(solution)/shard_map/ppermute | solution.py:16
  72.5 1.7 reshape.246
  74.2 1.1 copy.127
  75.3 3.0 %reshape.250 = f32[2,2,256,273]{2,1,3,0:T(2,128)} reshape(f32[2,512,273]{1,2,0:T(8,128)} %get-tuple-element.279) | data formatting | bytes 2236416 | tf_op jit(solution)/shard_map/reshape | solution.py:167
  80.2 25.4 %while.21 = (s32[]{:T(128)}, f32[2,273,112]{2,1,0:T(8,128)S(1)}, f32[2,273]{0,1:T(8,128)S(1)}, s32[]{:T(128)}, bf16[2,2,256,112]{2,3,1,0:T(8,128)(2,1)}, /*index...) while((s32[]{:T(128)}, f32[2,273,112]{2,1,0:T(8,128)S(1)}, ...), condition=%wide.region_10.11_spmd, body=%wide.region_4.10_spmd.sunk | while | flops 1377437056 | bytes 23302216 | solution.py:182
  85.4 1.2 constant_dynamic-slice_fusion.7
  98.0 1.2 constant_dynamic-slice_fusion.7
  105.5 1.2 copy.96
  106.8 1.9 fusion.82
  108.7 2.0 add_convert_fusion
  110.8 1.1 constant_dynamic-slice_fusion.3
  111.9 15.2 %all_to_all.15 = bf16[32,2,8,224]{3,2,1,0:T(8,128)(2,1)S(1)} all-to-all(bf16[32,2,8,224]{3,2,1,0:T(8,128)(2,1)S(1)} %constant_dynamic-slice_fusion.3), channel_id=1, replica_groups=mesh['group'=32,'mp'=8] {'group'}, dimensions={0} | all-to-all | bytes 458752 | tf_op jit(solution)/shard_map/all_to_all | solution.py:122
  128.2 26.6 %reduce-scatter.2.cloned.1.call-done = bf16[512,224]{0,1:T(8,128)(2,1)} async-done(((bf16[512,1792]{0,1:T(8,128)(2,1)}), bf16[512,224]{0,1:T(8,128)(2,1)}) %reduce-scatter.2.cloned.1.call-update) | async-done | bytes 229392 | tf_op jit(solution)/shard_map/reduce_scatter | solution.py:206
  154.7 1.7 add_convert_fusion.1
  156.4 39.4 %all-gather.5.cloned.1.call-done = bf16[512,1792]{0,1:T(8,128)(2,1)} async-done(((bf16[512,224]{0,1:T(8,128)(2,1)}), bf16[512,1792]{0,1:T(8,128)(2,1)}) %all-gather.5.cloned.1.call-update) | async-done | bytes 1835024 | tf_op jit(solution)/shard_map/all_gather | solution.py:210
  195.8 3.2 %convolution_reduce_fusion = f32[512]{0:T(512)S(1)} fusion(bf16[512,1792]{1,0:T(8,128)(2,1)} %all-gather.3.cloned.1.call-done, bf16[512,1792]{0,1:T(8,128)(2,1)} %all-gather.5.cloned.1.call-done), kind=kOutput, calls=%fused_computation.82 | convolution fusion | flops 939785728 | bytes 3672064 | tf_op jit(solution)/shard_map/rd,vd->rv/dot_general | solution.py:79
  199.0 16.1 %pmax.7 = f32[512]{0:T(512)S(1)} all-reduce(f32[512]{0:T(512)S(1)} %convolution_reduce_fusion), channel_id=1, replica_groups=mesh['group'=32,'mp'=8] {'mp'}, use_global_device_ids=true, to_apply=%region_15.16 | all-reduce | flops 512 | bytes 4096 | tf_op jit(solution)/shard_map/pmax | solution.py:213
  (145 shorter events, 33.3 us)
Async XLA Ops:
  7.2 8.7 %copy-start = (bf16[512,1792]{1,0:T(8,128)(2,1)S(1)}, bf16[512,1792]{1,0:T(8,128)(2,1)}, u32[]{:S(2)}) copy-start(bf16[512,1792]{1,0:T(8,128)(2,1)} %param.13) | copy-start | bytes 5505028
  7.2 55.2 %all-gather.3.cloned.1.call-start = ((), (), s32[]{:S(2)}) async-start(), calls=%async_computation.4 | async-start | bytes 1892352 | tf_op jit(solution)/shard_map/all_gather | solution.py:138
  9.8 34.6 %collective-permute-start.2 = (bf16[1]{0:T(256)(128)(2,1)}, bf16[1]{0:T(256)(128)(2,1)}, u32[]{:S(2)}, u32[]{:S(2)}) collective-permute-start(bf16[1]{0:T(256)(128)(2,1)} %bitcast.33), channel_id=1, source_target_pairs={{0,8},{8,16},{16,24},{24,32},{32,40},{40,48},{48,56},{56,64},{64,7... | collective-permute-start | bytes 14 | tf_op jit(solution)/shard_map/ppermute | solution.py:16
  17.8 2.1 copy-start.14
  20.0 11.9 %copy-start.8 = (s32[512]{0:T(512)S(1)}, s32[512]{0:T(512)}, u32[]{:S(2)}) copy-start(s32[512]{0:T(512)} %param.20) | copy-start | bytes 6148
  20.0 11.9 %copy-start.11 = (s32[128]{0:T(128)S(1)}, s32[128]{0:T(128)}, u32[]{:S(2)}) copy-start(s32[128]{0:T(128)} %param.21) | copy-start | bytes 1540
  20.0 12.8 %copy-start.13 = (bf16[1792,288]{0,1:T(8,128)(2,1)S(1)}, bf16[1792,288]{0,1:T(8,128)(2,1)}, u32[]{:S(2)}) copy-start(bf16[1792,288]{0,1:T(8,128)(2,1)} %param.15) | copy-start | bytes 3096580
  23.0 15.2 %all-to-all-start.1 = ((bf16[32,2,8,128]{3,2,1,0:T(8,128)(2,1)}), bf16[32,2,8,128]{3,2,1,0:T(8,128)(2,1)S(1)}, u32[]{:S(2)}, u32[]{:S(2)}) async-start(bf16[32,2,8,128]{3,2,1,0:T(8,128)(2,1)} %fusion.59), calls=%async_computation.1 | async-start | bytes 262144 | tf_op jit(solution)/shard_map/all_to_all | solution.py:124
  32.8 3.5 %copy-start.12 = (s32[64]{0:T(128)S(1)}, s32[64]{0:T(128)}, u32[]{:S(2)}) copy-start(s32[64]{0:T(128)} %param.22) | copy-start | bytes 772
  36.3 26.4 %copy-start.9 = (s32[1024]{0:T(1024)}, s32[1024]{0:T(1024)S(1)}, u32[]{:S(2)}) copy-start(s32[1024]{0:T(1024)S(1)} %pad_clamp_fusion) | copy-start | bytes 12292
  38.2 14.3 %all-to-all-start = ((bf16[32,2,8,288]{3,2,1,0:T(8,128)(2,1)}), bf16[32,2,8,288]{3,2,1,0:T(8,128)(2,1)S(1)}, u32[]{:S(2)}, u32[]{:S(2)}) async-start(bf16[32,2,8,288]{3,2,1,0:T(8,128)(2,1)} %fusion.56), calls=%async_computation | async-start | bytes 786432 | tf_op jit(solution)/shard_map/all_to_all | solution.py:123
  43.8 110.9 %reduce-scatter.2.cloned.1.call-start = ((), (), s32[]{:S(2)}) async-start(), calls=%async_computation.5 | async-start | bytes 2064384 | tf_op jit(solution)/shard_map/reduce_scatter | solution.py:206
  66.5 11.8 %collective-permute-start.1 = (bf16[2,273]{0,1:T(8,128)(2,1)S(1)}, bf16[2,273]{0,1:T(8,128)(2,1)}, u32[]{:S(2)}, u32[]{:S(2)}) collective-permute-start(bf16[2,273]{0,1:T(8,128)(2,1)S(1)} %bitcast.252), channel_id=1, source_target_pairs={{0,8},{8,16},{16,24},{24,32},{32,40},{40,48},{48,56},{56,64},{64,7... | collective-permute-start | bytes 3284 | tf_op jit(solution)/shard_map/ppermute | solution.py:16
  68.6 10.6 %collective-permute-start = (bf16[2,273,112]{2,1,0:T(8,128)(2,1)}, bf16[2,273,112]{2,1,0:T(8,128)(2,1)}, u32[]{:S(2)}, u32[]{:S(2)}) collective-permute-start(bf16[2,273,112]{2,1,0:T(8,128)(2,1)} %convolution_convert_fusion), channel_id=1, source_target_pairs={{0,8},{8,16},{16,24},{24,32},{32,40},{40,48},{48,56},{56,64},{64,7... | collective-permute-start | bytes 366920 | tf_op jit(solution)/shard_map/ppermute | solution.py:16
  74.2 5.9 %copy-start.7 = (f32[2,2,256,16]{2,3,1,0:T(8,128)S(1)}, f32[2,2,256,16]{2,3,1,0:T(8,128)}, u32[]{:S(2)}) copy-start(f32[2,2,256,16]{2,3,1,0:T(8,128)} %get-tuple-element.383) | copy-start | bytes 196612
  82.8 2.6 %copy-start.1 = (f32[2,2,256,273]{2,0,3,1:T(2,128)S(1)}, f32[2,2,256,273]{2,0,3,1:T(2,128)}, u32[]{:S(2)}) copy-start(f32[2,2,256,273]{2,0,3,1:T(2,128)} %get-tuple-element.411) | copy-start | bytes 3354628 | tf_op jit(solution)/shard_map/while
  82.8 2.6 %copy-start.2 = (f32[2,2,256,273]{2,0,3,1:T(2,128)S(1)}, f32[2,2,256,273]{2,0,3,1:T(2,128)}, u32[]{:S(2)}) copy-start(f32[2,2,256,273]{2,0,3,1:T(2,128)} %get-tuple-element.415) | copy-start | bytes 3354628 | tf_op jit(solution)/shard_map/while
  85.4 2.5 %copy-start.5 = (bf16[2,2,256,112]{2,3,1,0:T(8,128)(2,1)S(1)}, bf16[2,2,256,112]{2,3,1,0:T(8,128)(2,1)}, u32[]{:S(2)}) copy-start(bf16[2,2,256,112]{2,3,1,0:T(8,128)(2,1)} %get-tuple-element.393) | copy-start | bytes 688132 | tf_op jit(solution)/shard_map/while
  88.4 3.8 %copy-start.6 = (bf16[2,2,256,112]{2,3,1,0:T(8,128)(2,1)}, bf16[2,2,256,112]{2,3,1,0:T(8,128)(2,1)S(1)}, u32[]{:S(2)}) copy-start(bf16[2,2,256,112]{2,3,1,0:T(8,128)(2,1)S(1)} %fusion.140) | copy-start | bytes 688132 | tf_op jit(solution)/shard_map/while
  95.4 2.6 %copy-start.1 = (f32[2,2,256,273]{2,0,3,1:T(2,128)S(1)}, f32[2,2,256,273]{2,0,3,1:T(2,128)}, u32[]{:S(2)}) copy-start(f32[2,2,256,273]{2,0,3,1:T(2,128)} %get-tuple-element.411) | copy-start | bytes 3354628 | tf_op jit(solution)/shard_map/while
  95.5 2.6 %copy-start.2 = (f32[2,2,256,273]{2,0,3,1:T(2,128)S(1)}, f32[2,2,256,273]{2,0,3,1:T(2,128)}, u32[]{:S(2)}) copy-start(f32[2,2,256,273]{2,0,3,1:T(2,128)} %get-tuple-element.415) | copy-start | bytes 3354628 | tf_op jit(solution)/shard_map/while
  98.0 2.5 %copy-start.5 = (bf16[2,2,256,112]{2,3,1,0:T(8,128)(2,1)S(1)}, bf16[2,2,256,112]{2,3,1,0:T(8,128)(2,1)}, u32[]{:S(2)}) copy-start(bf16[2,2,256,112]{2,3,1,0:T(8,128)(2,1)} %get-tuple-element.393) | copy-start | bytes 688132 | tf_op jit(solution)/shard_map/while
  101.0 3.8 %copy-start.6 = (bf16[2,2,256,112]{2,3,1,0:T(8,128)(2,1)}, bf16[2,2,256,112]{2,3,1,0:T(8,128)(2,1)S(1)}, u32[]{:S(2)}) copy-start(bf16[2,2,256,112]{2,3,1,0:T(8,128)(2,1)S(1)} %fusion.140) | copy-start | bytes 688132 | tf_op jit(solution)/shard_map/while
  106.7 1.9 copy-start.3
  106.8 1.9 copy-start.4
  106.8 1.9 copy-start.10
  110.7 85.1 %all-gather.5.cloned.1.call-start = ((), (), s32[]{:S(2)}) async-start(), calls=%async_computation.6 | async-start | bytes 2064384 | tf_op jit(solution)/shard_map/all_gather | solution.py:210
Sparse Core Ops, SparseCore 0:
  10.6 51.8 all-gather.2
  110.9 43.7 reduce-scatter.1
  156.5 39.2 all-gather.4
where the time goes:
time: 223 us; the launch traced here: 222 us
  waiting for transfers between devices  83.9 us (38%)
  matrix products  31.4 us (14%)
  blocking collectives  31.4 us (14%)
  local copies, waits for them, and re-layouts  23.3 us (10%)
  starting transfers between devices  21.5 us (10%)
  between operations  15.5 us (7%)
  other arithmetic  12.4 us (6%)
  loops' own time  2.93 us (1%)
    all_gather x1, waiting for transfers between devices, on_device(): group_rows = lax.all_gather(final_rows, 'mp', axis=1, tiled=True)  39.4 us
    reduce_scatter x1, waiting for transfers between devices, on_device(): lax.psum_scatter(partial_value.astype(jnp.bfloat16), 'mp', scatter_dimens...  26.6 us
    pmax x1, blocking collectives, on_device(): lax.pmax(partial_best, 'mp')  16.1 us
    all_to_all x1, blocking collectives, on_device(): lax.all_to_all(kept_pages, 'group', split_axis=0, concat_axis=0, tiled=True)  15.2 us
    all_gather x1, waiting for transfers between devices, on_device(): group_vocab = lax.all_gather(vocab_rows, 'group', axis=0, tiled=True)  9.2 us
    all_to_all x1, starting transfers between devices, on_device(): lax.all_to_all(lowered_pages, 'group', split_axis=0, concat_axis=0, tiled...  8.52 us
    ppermute x3, starting transfers between devices, from_behind(): return lax.ppermute(value, axis, pairs)  7.28 us
    all_to_all x1, waiting for transfers between devices, on_device(): lax.all_to_all(projected_pages, 'group', split_axis=0, concat_axis=0, til...  6.21 us
  transfers between devices with their start and end apart: 8, of which 5 were waited for; matrix products, arithmetic and copies ran while one was open for 13% of the time, Pallas kernels for 0%

commit v1 on v0

--- a/solution.py
+++ b/solution.py
@@ -207,7 +207,11 @@
         partial_value.astype(jnp.bfloat16), "mp", scatter_dimension=1, tiled=True
     )
     final_rows = (residual.astype(jnp.float32) + summed.astype(jnp.float32)).astype(jnp.bfloat16)
-    group_rows = lax.all_gather(final_rows, "mp", axis=1, tiled=True)
+    size_2 = lax.axis_size("mp")
+    repeats = [size_2 if d == 1 else 1 for d in range(final_rows.ndim)]
+    group_rows = lax.all_to_all(
+        jnp.tile(final_rows, repeats), "mp", split_axis=1, concat_axis=1, tiled=True
+    )
     partial_best = best_of(group_rows, group_vocab)
     max_logits = lax.dynamic_slice_in_dim(
         lax.pmax(partial_best, "mp"), own_shard * (rows_here // shards), rows_here // shards

time: 223 us -> 229 us (1.027)
  starting transfers between devices: 21.5 us -> 25.9 us
  waiting for transfers between devices: 83.9 us -> 87.9 us
    all_to_all x0 -> x1, waiting for transfers between devices: none -> 42.7 us  [on_device(): lax.all_to_all(jnp.tile(final_rows, repeats), 'mp', split_axis=1, concat_...]
    all_gather x1 -> x0, waiting for transfers between devices: 39.4 us -> none  [on_device(): group_rows = lax.all_gather(final_rows, 'mp', axis=1, tiled=True)]
    all_to_all x0 -> x1, starting transfers between devices: none -> 4.39 us  [on_device(): lax.all_to_all(jnp.tile(final_rows, repeats), 'mp', split_axis=1, concat_...]
  transfers between devices with their start and end apart: 8 -> 8, of which waited for: 5 -> 5; matrix products, arithmetic and copies ran while one was open for 13% -> 12% of each run, Pallas kernels for 0% -> 0%
where the time goes in v1:
time: 229 us; the launch traced here: 228 us
  waiting for transfers between devices  87.9 us (38%)
  matrix products  30.2 us (13%)
  blocking collectives  29.9 us (13%)
  starting transfers between devices  25.9 us (11%)
  local copies, waits for them, and re-layouts  24.1 us (11%)
  between operations  15.7 us (7%)
  other arithmetic  11.2 us (5%)
  loops' own time  2.99 us (1%)
    all_to_all x1, waiting for transfers between devices, on_device(): lax.all_to_all(jnp.tile(final_rows, repeats), 'mp', split_axis=1, concat_...  42.7 us
    reduce_scatter x1, waiting for transfers between devices, on_device(): lax.psum_scatter(partial_value.astype(jnp.bfloat16), 'mp', scatter_dimens...  26.7 us
    all_to_all x1, blocking collectives, on_device(): lax.all_to_all(kept_pages, 'group', split_axis=0, concat_axis=0, tiled=True)  15.2 us
    pmax x1, blocking collectives, on_device(): lax.pmax(partial_best, 'mp')  14.7 us
    all_gather x1, waiting for transfers between devices, on_device(): group_vocab = lax.all_gather(vocab_rows, 'group', axis=0, tiled=True)  9.2 us
    all_to_all x1, starting transfers between devices, on_device(): lax.all_to_all(lowered_pages, 'group', split_axis=0, concat_axis=0, tiled...  8.38 us
    ppermute x3, starting transfers between devices, from_behind(): return lax.ppermute(value, axis, pairs)  7.44 us
    all_to_all x1, waiting for transfers between devices, on_device(): lax.all_to_all(projected_pages, 'group', split_axis=0, concat_axis=0, til...  6.82 us
  transfers between devices with their start and end apart: 8, of which 5 were waited for; matrix products, arithmetic and copies ran while one was open for 12% of the time, Pallas kernels for 0%

profile of v1, /device:TPU:2, one launch (start us, length us, event | category | flops | bytes accessed | tf_op | source)
XLA Modules:
  0.0 228.0 jit_solution(18089982502119221653)
XLA Ops:
  7.9 1.3 slice.34
  9.8 2.9 %collective-permute-start.2 = (bf16[1]{0:T(256)(128)(2,1)}, bf16[1]{0:T(256)(128)(2,1)}, u32[]{:S(2)}, u32[]{:S(2)}) collective-permute-start(bf16[1]{0:T(256)(128)(2,1)} %bitcast.33), channel_id=1, source_target_pairs={{0,8},{8,16},{16,24},{24,32},{32,40},{40,48},{48,56},{56,64},{64,7... | collective-permute-start | bytes 14 | tf_op jit(solution)/shard_map/ppermute | solution.py:16
  16.0 1.9 gather_fusion
  17.9 2.0 fusion.49
  20.1 3.0 %fusion.59 = bf16[32,2,8,128]{3,2,1,0:T(8,128)(2,1)} fusion(bf16[32,2,8,1792]{3,2,1,0:T(8,128)(2,1)} %bitcast.227, f32[1792]{0:T(1024)S(1)} %copy-done.13, f32[32,2,8]{2,1,0:T(2,128)S(1)} %copy.90, bf16[1792,128]{1,0:T(8,128)(2,1)} %param.17), kind=kOutput, calls=%fused_computation.84 | convolution fusion | flops 238616576 | bytes 2434048 | tf_op jit(solution)/shard_map/abrd,dc->abrc/dot_general | solution.py:117
  23.1 8.4 %all-to-all-start.1 = ((bf16[32,2,8,128]{3,2,1,0:T(8,128)(2,1)}), bf16[32,2,8,128]{3,2,1,0:T(8,128)(2,1)S(1)}, u32[]{:S(2)}, u32[]{:S(2)}) async-start(bf16[32,2,8,128]{3,2,1,0:T(8,128)(2,1)} %fusion.59), calls=%async_computation.1 | async-start | bytes 262144 | tf_op jit(solution)/shard_map/all_to_all | solution.py:124
  32.8 3.4 %fusion.56 = bf16[32,2,8,288]{3,2,1,0:T(8,128)(2,1)} fusion(bf16[32,2,8,1792]{3,2,1,0:T(8,128)(2,1)} %bitcast.228, f32[1792]{0:T(1024)S(1)} %copy-done.13, f32[32,2,8]{2,1,0:T(2,128)S(1)} %copy.90, bf16[1792,288]{0,1:T(8,128)(2,1)S(1)} %copy-done.12), kind=kOutput, calls=%fused_computation.81 | convolution fusion | flops 532299776 | bytes 3171328 | tf_op jit(solution)/shard_map/abrd,dc->abrc/dot_general | solution.py:114
  36.4 1.8 all-to-all-done.1
  38.2 5.6 %all-to-all-start = ((bf16[32,2,8,288]{3,2,1,0:T(8,128)(2,1)}), bf16[32,2,8,288]{3,2,1,0:T(8,128)(2,1)S(1)}, u32[]{:S(2)}, u32[]{:S(2)}) async-start(bf16[32,2,8,288]{3,2,1,0:T(8,128)(2,1)} %fusion.56), calls=%async_computation | async-start | bytes 786432 | tf_op jit(solution)/shard_map/all_to_all | solution.py:123
  44.5 1.3 gather_fusion.2
  45.7 6.8 %all-to-all-done = bf16[32,2,8,288]{3,2,1,0:T(8,128)(2,1)S(1)} async-done(((bf16[32,2,8,288]{3,2,1,0:T(8,128)(2,1)}), bf16[32,2,8,288]{3,2,1,0:T(8,128)(2,1)S(1)}, u32[]{:S(2)}, u32[]{:S(2)}) %all-to-all-start) | async-done | bytes 294944 | tf_op jit(solution)/shard_map/all_to_all | solution.py:123
  53.2 9.2 %all-gather.2.cloned.1.call-done = bf16[512,1792]{1,0:T(8,128)(2,1)} async-done(((bf16[16,1792]{1,0:T(8,128)(2,1)}), bf16[512,1792]{1,0:T(8,128)(2,1)}) %all-gather.2.cloned.1.call-update) | async-done | bytes 1835024 | tf_op jit(solution)/shard_map/all_gather | solution.py:138
  63.0 1.3 pad_maximum_fusion.1
  64.3 1.3 convolution_convert_fusion
  67.1 2.2 collective-permute-start.1
  69.3 2.4 %collective-permute-start = (bf16[2,273,112]{2,1,0:T(8,128)(2,1)}, bf16[2,273,112]{2,1,0:T(8,128)(2,1)}, u32[]{:S(2)}, u32[]{:S(2)}) collective-permute-start(bf16[2,273,112]{2,1,0:T(8,128)(2,1)} %convolution_convert_fusion), channel_id=1, source_target_pairs={{0,8},{8,16},{16,24},{24,32},{32,40},{40,48},{48,56},{56,64},{64,7... | collective-permute-start | bytes 366920 | tf_op jit(solution)/shard_map/ppermute | solution.py:16
  73.2 1.7 reshape.253
  74.9 3.0 %reshape.257 = f32[2,2,256,273]{2,1,3,0:T(2,128)} reshape(f32[2,512,273]{1,2,0:T(8,128)} %get-tuple-element.279) | data formatting | bytes 2236416 | tf_op jit(solution)/shard_map/reshape | solution.py:167
  79.8 24.3 %while.21 = (s32[]{:T(128)}, f32[2,273,112]{2,1,0:T(8,128)S(1)}, f32[2,273]{0,1:T(8,128)S(1)}, s32[]{:T(128)}, bf16[2,2,256,112]{2,3,1,0:T(8,128)(2,1)}, /*index...) while((s32[]{:T(128)}, f32[2,273,112]{2,1,0:T(8,128)S(1)}, ...), condition=%wide.region_10.11_spmd, body=%wide.region_4.10_spmd.sunk | while | flops 1377437056 | bytes 23302216 | solution.py:182
  85.0 1.2 constant_dynamic-slice_fusion.7
  97.1 1.2 constant_dynamic-slice_fusion.7
  104.1 1.2 copy.97
  105.3 1.9 fusion.82
  107.2 2.0 add_convert_fusion
  109.3 1.1 constant_dynamic-slice_fusion.3
  110.4 15.2 %all_to_all.24 = bf16[32,2,8,224]{3,2,1,0:T(8,128)(2,1)S(1)} all-to-all(bf16[32,2,8,224]{3,2,1,0:T(8,128)(2,1)S(1)} %constant_dynamic-slice_fusion.3), channel_id=1, replica_groups=mesh['group'=32,'mp'=8] {'group'}, dimensions={0} | all-to-all | bytes 458752 | tf_op jit(solution)/shard_map/all_to_all | solution.py:122
  126.5 26.7 %reduce-scatter.2.cloned.1.call-done = bf16[512,224]{0,1:T(8,128)(2,1)} async-done(((bf16[512,1792]{0,1:T(8,128)(2,1)}), bf16[512,224]{0,1:T(8,128)(2,1)}) %reduce-scatter.2.cloned.1.call-update) | async-done | bytes 229392 | tf_op jit(solution)/shard_map/reduce_scatter | solution.py:206
  154.2 1.4 tile.2
  155.6 4.4 %all-to-all-start.3 = ((bf16[512,8,224]{0,2,1:T(8,128)(2,1)}), bf16[512,8,224]{0,2,1:T(8,128)(2,1)}, u32[]{:S(2)}, u32[]{:S(2)}) async-start(bf16[512,8,224]{0,2,1:T(8,128)(2,1)} %tile.2), calls=%async_computation.4 | async-start | bytes 3670016 | tf_op jit(solution)/shard_map/all_to_all | solution.py:212
  160.0 42.7 %all-to-all-done.3 = bf16[512,8,224]{0,2,1:T(8,128)(2,1)} async-done(((bf16[512,8,224]{0,2,1:T(8,128)(2,1)}), bf16[512,8,224]{0,2,1:T(8,128)(2,1)}, u32[]{:S(2)}, u32[]{:S(2)}) %all-to-all-start.3) | async-done | bytes 1835040 | tf_op jit(solution)/shard_map/all_to_all | solution.py:212
  202.7 3.2 %convolution_reduce_fusion = f32[512]{0:T(512)S(1)} fusion(bf16[512,1792]{1,0:T(8,128)(2,1)} %all-gather.2.cloned.1.call-done, bf16[512,1792]{0,1:T(8,128)(2,1)} %bitcast.50), kind=kOutput, calls=%fused_computation.82 | convolution fusion | flops 939785728 | bytes 3672064 | tf_op jit(solution)/shard_map/rd,vd->rv/dot_general | solution.py:79
  205.8 14.7 %pmax.7 = f32[512]{0:T(512)S(1)} all-reduce(f32[512]{0:T(512)S(1)} %convolution_reduce_fusion), channel_id=1, replica_groups=mesh['group'=32,'mp'=8] {'mp'}, use_global_device_ids=true, to_apply=%region_15.16 | all-reduce | flops 512 | bytes 4096 | tf_op jit(solution)/shard_map/pmax | solution.py:217
  (145 shorter events, 33.1 us)
Async XLA Ops:
  7.2 8.9 %copy-start = (bf16[512,1792]{1,0:T(8,128)(2,1)S(1)}, bf16[512,1792]{1,0:T(8,128)(2,1)}, u32[]{:S(2)}) copy-start(bf16[512,1792]{1,0:T(8,128)(2,1)} %param.13) | copy-start | bytes 5505028
  7.2 55.2 %all-gather.2.cloned.1.call-start = ((), (), s32[]{:S(2)}) async-start(), calls=%async_computation.5 | async-start | bytes 1892352 | tf_op jit(solution)/shard_map/all_gather | solution.py:138
  9.8 34.1 %collective-permute-start.2 = (bf16[1]{0:T(256)(128)(2,1)}, bf16[1]{0:T(256)(128)(2,1)}, u32[]{:S(2)}, u32[]{:S(2)}) collective-permute-start(bf16[1]{0:T(256)(128)(2,1)} %bitcast.33), channel_id=1, source_target_pairs={{0,8},{8,16},{16,24},{24,32},{32,40},{40,48},{48,56},{56,64},{64,7... | collective-permute-start | bytes 14 | tf_op jit(solution)/shard_map/ppermute | solution.py:16
  17.9 2.1 copy-start.13
  20.1 11.8 %copy-start.9 = (s32[512]{0:T(512)S(1)}, s32[512]{0:T(512)}, u32[]{:S(2)}) copy-start(s32[512]{0:T(512)} %param.20) | copy-start | bytes 6148
  20.1 11.8 %copy-start.10 = (s32[128]{0:T(128)S(1)}, s32[128]{0:T(128)}, u32[]{:S(2)}) copy-start(s32[128]{0:T(128)} %param.21) | copy-start | bytes 1540
  20.1 12.7 %copy-start.12 = (bf16[1792,288]{0,1:T(8,128)(2,1)S(1)}, bf16[1792,288]{0,1:T(8,128)(2,1)}, u32[]{:S(2)}) copy-start(bf16[1792,288]{0,1:T(8,128)(2,1)} %param.15) | copy-start | bytes 3096580
  23.1 15.1 %all-to-all-start.1 = ((bf16[32,2,8,128]{3,2,1,0:T(8,128)(2,1)}), bf16[32,2,8,128]{3,2,1,0:T(8,128)(2,1)S(1)}, u32[]{:S(2)}, u32[]{:S(2)}) async-start(bf16[32,2,8,128]{3,2,1,0:T(8,128)(2,1)} %fusion.59), calls=%async_computation.1 | async-start | bytes 262144 | tf_op jit(solution)/shard_map/all_to_all | solution.py:124
  32.8 3.5 %copy-start.11 = (s32[64]{0:T(128)S(1)}, s32[64]{0:T(128)}, u32[]{:S(2)}) copy-start(s32[64]{0:T(128)} %param.22) | copy-start | bytes 772
  38.2 14.3 %all-to-all-start = ((bf16[32,2,8,288]{3,2,1,0:T(8,128)(2,1)}), bf16[32,2,8,288]{3,2,1,0:T(8,128)(2,1)S(1)}, u32[]{:S(2)}, u32[]{:S(2)}) async-start(bf16[32,2,8,288]{3,2,1,0:T(8,128)(2,1)} %fusion.56), calls=%async_computation | async-start | bytes 786432 | tf_op jit(solution)/shard_map/all_to_all | solution.py:123
  43.8 109.4 %reduce-scatter.2.cloned.1.call-start = ((), (), s32[]{:S(2)}) async-start(), calls=%async_computation.6 | async-start | bytes 2064384 | tf_op jit(solution)/shard_map/reduce_scatter | solution.py:206
  67.1 10.8 %collective-permute-start.1 = (bf16[2,273]{0,1:T(8,128)(2,1)}, bf16[2,273]{0,1:T(8,128)(2,1)}, u32[]{:S(2)}, u32[]{:S(2)}) collective-permute-start(bf16[2,273]{0,1:T(8,128)(2,1)} %bitcast.141), channel_id=1, source_target_pairs={{0,8},{8,16},{16,24},{24,32},{32,40},{40,48},{48,56},{56,64},{64,7... | collective-permute-start | bytes 3284 | tf_op jit(solution)/shard_map/ppermute | solution.py:16
  69.3 9.6 %collective-permute-start = (bf16[2,273,112]{2,1,0:T(8,128)(2,1)}, bf16[2,273,112]{2,1,0:T(8,128)(2,1)}, u32[]{:S(2)}, u32[]{:S(2)}) collective-permute-start(bf16[2,273,112]{2,1,0:T(8,128)(2,1)} %convolution_convert_fusion), channel_id=1, source_target_pairs={{0,8},{8,16},{16,24},{24,32},{32,40},{40,48},{48,56},{56,64},{64,7... | collective-permute-start | bytes 366920 | tf_op jit(solution)/shard_map/ppermute | solution.py:16
  73.2 1.7 copy-start.3
  74.9 4.9 %copy-start.8 = (f32[2,2,256,16]{2,3,1,0:T(8,128)S(1)}, f32[2,2,256,16]{2,3,1,0:T(8,128)}, u32[]{:S(2)}) copy-start(f32[2,2,256,16]{2,3,1,0:T(8,128)} %get-tuple-element.383) | copy-start | bytes 196612
  82.4 2.6 %copy-start.1 = (f32[2,2,256,273]{2,0,3,1:T(2,128)S(1)}, f32[2,2,256,273]{2,0,3,1:T(2,128)}, u32[]{:S(2)}) copy-start(f32[2,2,256,273]{2,0,3,1:T(2,128)} %get-tuple-element.411) | copy-start | bytes 3354628 | tf_op jit(solution)/shard_map/while
  82.4 2.6 %copy-start.2 = (f32[2,2,256,273]{2,0,3,1:T(2,128)S(1)}, f32[2,2,256,273]{2,0,3,1:T(2,128)}, u32[]{:S(2)}) copy-start(f32[2,2,256,273]{2,0,3,1:T(2,128)} %get-tuple-element.415) | copy-start | bytes 3354628 | tf_op jit(solution)/shard_map/while
  85.0 2.5 %copy-start.6 = (bf16[2,2,256,112]{2,3,1,0:T(8,128)(2,1)S(1)}, bf16[2,2,256,112]{2,3,1,0:T(8,128)(2,1)}, u32[]{:S(2)}) copy-start(bf16[2,2,256,112]{2,3,1,0:T(8,128)(2,1)} %get-tuple-element.393) | copy-start | bytes 688132 | tf_op jit(solution)/shard_map/while
  88.0 3.3 %copy-start.7 = (bf16[2,2,256,112]{2,3,1,0:T(8,128)(2,1)}, bf16[2,2,256,112]{2,3,1,0:T(8,128)(2,1)S(1)}, u32[]{:S(2)}) copy-start(bf16[2,2,256,112]{2,3,1,0:T(8,128)(2,1)S(1)} %fusion.140) | copy-start | bytes 688132 | tf_op jit(solution)/shard_map/while
  94.5 2.6 %copy-start.1 = (f32[2,2,256,273]{2,0,3,1:T(2,128)S(1)}, f32[2,2,256,273]{2,0,3,1:T(2,128)}, u32[]{:S(2)}) copy-start(f32[2,2,256,273]{2,0,3,1:T(2,128)} %get-tuple-element.411) | copy-start | bytes 3354628 | tf_op jit(solution)/shard_map/while
  94.6 2.6 %copy-start.2 = (f32[2,2,256,273]{2,0,3,1:T(2,128)S(1)}, f32[2,2,256,273]{2,0,3,1:T(2,128)}, u32[]{:S(2)}) copy-start(f32[2,2,256,273]{2,0,3,1:T(2,128)} %get-tuple-element.415) | copy-start | bytes 3354628 | tf_op jit(solution)/shard_map/while
  97.1 2.5 %copy-start.6 = (bf16[2,2,256,112]{2,3,1,0:T(8,128)(2,1)S(1)}, bf16[2,2,256,112]{2,3,1,0:T(8,128)(2,1)}, u32[]{:S(2)}) copy-start(bf16[2,2,256,112]{2,3,1,0:T(8,128)(2,1)} %get-tuple-element.393) | copy-start | bytes 688132 | tf_op jit(solution)/shard_map/while
  100.1 3.3 %copy-start.7 = (bf16[2,2,256,112]{2,3,1,0:T(8,128)(2,1)}, bf16[2,2,256,112]{2,3,1,0:T(8,128)(2,1)S(1)}, u32[]{:S(2)}) copy-start(bf16[2,2,256,112]{2,3,1,0:T(8,128)(2,1)S(1)} %fusion.140) | copy-start | bytes 688132 | tf_op jit(solution)/shard_map/while
  104.1 3.2 %copy-start.14 = (f32[2,2,256]{2,1,0:T(2,128)}, f32[2,2,256]{2,1,0:T(2,128)S(1)}, u32[]{:S(2)}) copy-start(f32[2,2,256]{2,1,0:T(2,128)S(1)} %get-tuple-element.189) | copy-start | bytes 12292
  105.3 1.9 copy-start.4
  105.3 1.9 copy-start.5
  155.6 47.1 %all-to-all-start.3 = ((bf16[512,8,224]{0,2,1:T(8,128)(2,1)}), bf16[512,8,224]{0,2,1:T(8,128)(2,1)}, u32[]{:S(2)}, u32[]{:S(2)}) async-start(bf16[512,8,224]{0,2,1:T(8,128)(2,1)} %tile.2), calls=%async_computation.4 | async-start | bytes 3670016 | tf_op jit(solution)/shard_map/all_to_all | solution.py:212
Sparse Core Ops, SparseCore 0:
  10.6 51.8 all-gather.1
  109.4 43.7 reduce-scatter.1
